TPU v7x, 128 devices: a whole 4x4x4 slice. The times are simulated.
128 devices in a mesh: seq: 8 (over y, core), tile: 16 (over z, x).
Axes of the slice: x: 4, y: 4, z: 4, core: 2. Of those that a mesh axis runs over, the one named last changes fastest.
Arguments:
- latents: bfloat16 [16384, 128], P(('seq', 'tile')), may hold values from -6 to 6
- grid_slot: int32 [16384], P(('seq', 'tile')), may hold values from 0 to 16383, as said below
- w_in: bfloat16 [432, 384], replicated, may hold values from -0.3125 to 0.3125
- b_in: float32 [384], replicated, may hold values from -3 to 3
- gain_in: float32 [384], replicated, may hold values from 0.1 to 1.9
- w_up: bfloat16 [3456, 192], replicated, may hold values from -0.109375 to 0.109375
- b_up: float32 [192], replicated, may hold values from -3 to 3
- gain_res: float32 [192], replicated, may hold values from 0.1 to 1.9
- w_res: bfloat16 [5184, 192], replicated, may hold values from -0.078125 to 0.078125
- b_res: float32 [192], replicated, may hold values from -3 to 3
Outputs:
- decoded: bfloat16 [16, 128, 49152], P(None, 'tile', 'seq')
Inputs may be any that keep to these rules, and one draw needn't show every extreme that they name: grid_slot is a permutation of 0 to 16383. Row r of the sequence lies on device r // 128 and grid row p on device p // 128 (devices in the order seq then tile). The rows of one device go to exactly 64 receiving devices, exactly 2 rows to each, so every device receives 128 rows; the receivers of device d are d + k modulo 128 for a set of offsets k common to all devices, which includes 128 / 2.
All inputs are finite; a program needn't handle non-finite values.
Results may differ from a plain program's by a relative error of at most 0.0058.
Values may be sent and summed in bfloat16 or wider, within the bound.
No kernel may reach another device: no remote copies, remote signals or barrier semaphores. Data moves between devices by JAX's collectives and lax.ppermute only.
A program may use at most 192 MiB of HBM per device.

v0:
```python
import jax
import jax.numpy as jnp
from jax import lax
from jax.sharding import PartitionSpec as P

LAT = 16
C1 = 384
C2 = 192
FS = 2
TH = 4
W = 128


def extended_2(block, sides, width):
    for axis, dim in sides:
        count = lax.axis_size(axis)
        forward = [(i, i + 1) for i in range(count - 1)]
        backward = [(target, source) for source, target in forward]
        low = lax.ppermute(
            lax.slice_in_dim(block, block.shape[dim] - width, None, axis=dim), axis, forward
        )
        high = lax.ppermute(lax.slice_in_dim(block, 0, width, axis=dim), axis, backward)
        block = jnp.concatenate([low, block, high], axis=dim)
    return block


def from_behind(x, axis, by):
    length = lax.axis_size(axis)
    pairs = [(i, i + by) for i in range(length) if 0 <= i + by < length]
    return lax.ppermute(x, axis, pairs)


def causal_taps(padded, weight, bias):
    frames = padded.shape[0] - 2
    height = padded.shape[1] - 2
    breadth = padded.shape[2] - 2
    channels = padded.shape[3]
    running = jnp.zeros((frames * height * breadth, weight.shape[1]), jnp.float32)
    for time_off in range(3):
        for row_off in range(3):
            window = jnp.concatenate(
                [
                    padded[
                        time_off : time_off + frames,
                        row_off : row_off + height,
                        col_off : col_off + breadth,
                    ]
                    for col_off in range(3)
                ],
                axis=-1,
            )
            start = (time_off * 3 + row_off) * 3 * channels
            running = running + jnp.dot(
                window.reshape(-1, 3 * channels),
                weight[start : start + 3 * channels],
                preferred_element_type=jnp.float32,
            )
    return (running + bias).reshape(frames, height, breadth, weight.shape[1])


def upsample_conv(extended, weight, bias):
    doubled = jnp.repeat(jnp.repeat(extended, 2, axis=1), 2, axis=2)[:, 1:-1, 1:-1]
    frames = doubled.shape[0]
    height = doubled.shape[1] - 2
    breadth = doubled.shape[2] - 2
    channels = doubled.shape[3]
    running = jnp.zeros((frames * height * breadth, weight.shape[1]), jnp.float32)
    for row_off in range(3):
        window = jnp.concatenate(
            [
                doubled[:, row_off : row_off + height, col_off : col_off + breadth]
                for col_off in range(3)
            ],
            axis=-1,
        )
        start = row_off * 3 * channels
        running = running + jnp.dot(
            window.reshape(-1, 3 * channels),
            weight[start : start + 3 * channels],
            preferred_element_type=jnp.float32,
        )
    return (running + bias).astype(jnp.bfloat16).reshape(frames, height, breadth, weight.shape[1])


def normed_silu(values, gain):
    scaled = values * lax.rsqrt(jnp.mean(values * values, axis=-1, keepdims=True) + 1e-06) * gain
    return jax.nn.silu(scaled).astype(jnp.bfloat16)


def local(latents, grid_slot, w_in, b_in, gain_in, w_up, b_up, gain_res, w_res, b_res):
    seq_count = lax.axis_size("seq")
    tile_count = lax.axis_size("tile")
    device_count = seq_count * tile_count
    row_count = latents.shape[0]
    row_width = latents.shape[1]
    slot_cap = 2 * row_count // device_count
    target = grid_slot // row_count
    local_row = grid_slot % row_count
    one_hot = (target[:, None] == jnp.arange(device_count, dtype=jnp.int32)[None, :]).astype(
        jnp.int32
    )
    rank_in = jnp.sum((jnp.cumsum(one_hot, axis=0) - 1) * one_hot, axis=1)
    send_slot = target * slot_cap + rank_in
    outbox = (
        jnp.zeros((device_count * slot_cap, row_width), latents.dtype).at[send_slot].set(latents)
    )
    labels = jnp.full((device_count * slot_cap,), row_count, jnp.int32).at[send_slot].set(local_row)
    inbox_rows, inbox_labels = (
        lax.all_to_all(
            outbox.reshape(device_count, slot_cap, row_width),
            ("seq", "tile"),
            split_axis=0,
            concat_axis=0,
            tiled=True,
        ),
        lax.all_to_all(
            labels.reshape(device_count, slot_cap),
            ("seq", "tile"),
            split_axis=0,
            concat_axis=0,
            tiled=True,
        ),
    )
    grid_rows = (
        jnp.zeros((row_count, row_width), jnp.bfloat16)
        .at[inbox_labels.reshape(-1)]
        .set(inbox_rows.reshape(-1, row_width), mode="drop")
    )
    grid_latent = grid_rows.reshape(FS, TH, W * LAT)
    extended = extended_2(grid_latent, (("tile", 1),), 1)
    before = from_behind(extended, "seq", 1)
    window_in = jnp.concatenate([before, extended], axis=0).reshape(FS + 2, TH + 2, W, LAT)
    window_in = jnp.pad(window_in, ((0, 0), (0, 0), (1, 1), (0, 0)))
    first_conv = causal_taps(window_in, w_in, b_in)
    first_act = normed_silu(first_conv, gain_in)
    act_ext = extended_2(first_act.reshape(FS, TH, W * C1), (("tile", 1),), 1)
    act_ext = jnp.pad(act_ext.reshape(FS, TH + 2, W, C1), ((0, 0), (0, 0), (1, 1), (0, 0)))
    section_out = upsample_conv(act_ext, w_up, b_up)
    upsampled = lax.all_to_all(
        section_out.reshape(FS, 2 * TH, 2 * W * C2), "seq", split_axis=2, concat_axis=0, tiled=True
    )
    upsampled = upsampled.reshape(FS * seq_count, 2 * TH, 2 * W // seq_count, C2)
    res_act = normed_silu(upsampled.astype(jnp.float32), gain_res)
    res_ext = extended_2(res_act, (("seq", 2), ("tile", 1)), 1)
    res_ext = jnp.pad(res_ext, ((2, 0), (0, 0), (0, 0), (0, 0)))
    res_conv = causal_taps(res_ext, w_res, b_res)
    decoded = (upsampled.astype(jnp.float32) + res_conv).astype(jnp.bfloat16)
    return decoded.reshape(decoded.shape[0], 2 * TH, -1)


def solution(mesh):
    return jax.shard_map(
        local,
        mesh=mesh,
        in_specs=(
            P(("seq", "tile"), None),
            P(("seq", "tile")),
            P(),
            P(),
            P(),
            P(),
            P(),
            P(),
            P(),
            P(),
        ),
        out_specs=P(None, "tile", "seq"),
        check_vma=False,
    )
```

profile of v0, /device:TPU:7, one launch (start us, length us, event | category | flops | bytes accessed | tf_op | source)
XLA Modules:
  0.0 614.1 jit_solution(8333284277565260925)
XLA Ops:
  2.9 10.8 %all-to-all-start = ((s32[128,1,2]{2,1,0:T(1,128)}), s32[128,1,2]{2,1,0:T(1,128)S(1)}, u32[]{:S(2)}, u32[]{:S(2)}) async-start(s32[128,1,2]{2,1,0:T(1,128)} %bitcast), calls=%async_computation | async-start | bytes 131072 | tf_op jit(solution)/shard_map/all_to_all | solution.py:116
  15.4 6.2 %all-to-all-done = s32[128,1,2]{2,1,0:T(1,128)S(1)} async-done(((s32[128,1,2]{2,1,0:T(1,128)}), s32[128,1,2]{2,1,0:T(1,128)S(1)}, u32[]{:S(2)}, u32[]{:S(2)}) %all-to-all-start) | async-done | bytes 1056 | tf_op jit(solution)/shard_map/all_to_all | solution.py:116
  21.6 6.1 all-to-all-start.1
  29.1 6.5 %all-to-all-done.1 = bf16[128,2,128]{2,1,0:T(2,128)(2,1)S(1)} async-done(((bf16[128,2,128]{2,1,0:T(2,128)(2,1)}), bf16[128,2,128]{2,1,0:T(2,128)(2,1)S(1)}, u32[]{:S(2)}, u32[]{:S(2)}) %all-to-all-start.1) | async-done | bytes 65568 | tf_op jit(solution)/shard_map/all_to_all | solution.py:109
  36.9 2.4 collective-permute-start.1
  39.3 5.0 collective-permute-start
  45.2 4.3 collective-permute-start.2
  62.3 2.5 pad_maximum_fusion.22
  66.0 2.4 fusion.39
  71.8 2.6 pad_maximum_fusion.20
  79.0 2.4 fusion.45
  87.5 4.8 multiply_reduce_fusion.1
  95.8 4.5 fusion.17
  102.5 6.5 %collective-permute-start.3 = (bf16[2,1,49152]{2,0,1:T(2,128)(2,1)S(1)}, bf16[2,1,49152]{2,0,1:T(2,128)(2,1)S(1)}, u32[]{:S(2)}, u32[]{:S(2)}) collective-permute-start(bf16[2,1,49152]{2,0,1:T(2,128)(2,1)S(1)} %get-tuple-element.44), channel_id=1, source_target_pairs={{0,1},{1,2},{2,3},{3,4},{4,5},{5,6},{6,7},{7,8},{8,9},{9,10},{10,1... | collective-permute-start | bytes 589832 | tf_op jit(solution)/shard_map/ppermute | solution.py:19
  116.5 2.7 broadcast_in_dim.14
  119.1 20.7 %fusion.57 = (bf16[2,8,256,384]{3,0,2,1:T(2,128)(2,1)S(1)}, bf16[2,8,256,384]{3,0,2,1:T(2,128)(2,1)}, bf16[2,8,256,384]{3,0,2,1:T(2,128)(2,1)}, bf16[2,8,256,384...) fusion(bf16[2,12,260,384]{3,0,2,1:T(2,128)(2,1)S(1)} %bitcast.103), kind=kLoop, calls=%fused_computation.140 | loop fusion | bytes 56623104 | tf_op jit(solution)/shard_map/slice | solution.py:71
  139.9 30.7 %pad_maximum_fusion = bf16[2,8,256,1152]{3,0,2,1:T(2,128)(2,1)} fusion(bf16[2,8,256,384]{3,0,2,1:T(2,128)(2,1)S(1)} %get-tuple-element.11, bf16[2,8,256,384]{3,0,2,1:T(2,128)(2,1)S(1)} %get-tuple-element.12, bf16[2,8,256,384]{3,0,2,1:T(2,128)(2,1)S(1)} %get-tuple-element.13), kind=kLoop, calls=%fused_computation.3 | loop fusion | flops 28311552 | bytes 18874368 | tf_op jit(solution)/shard_map/concatenate | solution.py:69
  170.6 9.1 %copy.133 = bf16[2,8,256,1152]{3,2,1,0:T(8,128)(2,1)} copy(bf16[2,8,256,1152]{3,0,2,1:T(2,128)(2,1)} %pad_maximum_fusion) | data formatting | bytes 18874368 | tf_op jit(solution)/shard_map/concatenate | solution.py:69
  179.7 13.1 %pad_maximum_fusion.1 = bf16[2,8,256,1152]{3,0,2,1:T(2,128)(2,1)} fusion(bf16[2,8,256,384]{3,0,2,1:T(2,128)(2,1)} %get-tuple-element.8, bf16[2,8,256,384]{3,0,2,1:T(2,128)(2,1)} %get-tuple-element.9, bf16[2,8,256,384]{3,0,2,1:T(2,128)(2,1)} %get-tuple-element.10), kind=kLoop, calls=%fused_computation.4 | loop fusion | flops 28311552 | bytes 18874368 | tf_op jit(solution)/shard_map/concatenate | solution.py:69
  192.7 9.1 %copy.134 = bf16[2,8,256,1152]{3,2,1,0:T(8,128)(2,1)} copy(bf16[2,8,256,1152]{3,0,2,1:T(2,128)(2,1)} %pad_maximum_fusion.1) | data formatting | bytes 18874368 | tf_op jit(solution)/shard_map/concatenate | solution.py:69
  201.8 31.2 %pad_maximum_fusion.2 = bf16[2,8,256,1152]{3,0,2,1:T(2,128)(2,1)} fusion(bf16[2,8,256,384]{3,0,2,1:T(2,128)(2,1)} %get-tuple-element.6, bf16[2,8,256,384]{3,0,2,1:T(2,128)(2,1)} %get-tuple-element.7, bf16[2,8,256,384]{3,0,2,1:T(2,128)(2,1)S(1)} %get-tuple-element.5), kind=kLoop, calls=%fused_computation.5 | loop fusion | flops 28311552 | bytes 18874368 | tf_op jit(solution)/shard_map/concatenate | solution.py:69
  233.1 9.2 %copy.135 = bf16[2,8,256,1152]{3,2,1,0:T(8,128)(2,1)} copy(bf16[2,8,256,1152]{3,0,2,1:T(2,128)(2,1)} %pad_maximum_fusion.2) | data formatting | bytes 18874368 | tf_op jit(solution)/shard_map/concatenate | solution.py:69
  242.3 7.1 %fusion.20 = f32[4096,192]{0,1:T(8,128)S(1)} fusion(bf16[4096,1152]{1,0:T(8,128)(2,1)} %bitcast.119, bf16[3456,192]{0,1:T(8,128)(2,1)S(1)} %copy-done.18), kind=kOutput, calls=%fused_computation.58 | convolution fusion | flops 1811939328 | bytes 13025280 | tf_op jit(solution)/shard_map/dot_general | solution.py:77
  249.4 7.1 %convolution_add_fusion.8 = f32[4096,192]{0,1:T(8,128)S(1)} fusion(f32[4096,192]{0,1:T(8,128)S(1)} %fusion.20, bf16[4096,1152]{1,0:T(8,128)(2,1)} %bitcast.106, bf16[3456,192]{0,1:T(8,128)(2,1)S(1)} %copy-done.18), kind=kOutput, calls=%fused_computation.35 | convolution fusion | flops 1812725760 | bytes 16171008 | tf_op jit(solution)/shard_map/dot_general | solution.py:77
  256.5 4.4 fusion.10
  260.9 3.1 copy.136
  264.1 3.2 reshape_reshape.3
  267.3 44.1 %copy.137 = bf16[2,8,49152]{1,0,2:T(2,128)(2,1)} copy(bf16[2,8,49152]{2,1,0:T(8,128)(2,1)} %reshape_reshape.3) | data formatting | bytes 3145728 | tf_op jit(solution)/shard_map/reshape;reshape | solution.py:140
  311.4 29.3 %reshape.257 = bf16[8,2,49152]{2,1,0:T(2,128)(2,1)S(1)} reshape(bf16[49152,2,8]{2,1,0:T(2,128)(2,1)} %bitcast.104) | data formatting | bytes 3145728
  340.7 24.8 %all_to_all.23 = bf16[8,2,49152]{2,1,0:T(2,128)(2,1)S(1)} all-to-all(bf16[8,2,49152]{2,1,0:T(2,128)(2,1)S(1)} %reshape.257), channel_id=1, replica_groups=mesh['seq'=8,'tile'=16] {'seq'}, dimensions={0} | all-to-all | bytes 3145728 | tf_op jit(solution)/shard_map/all_to_all | solution.py:139
  365.5 31.8 %reshape.258 = bf16[49152,2,8]{2,1,0:T(2,128)(2,1)} reshape(bf16[8,2,49152]{2,1,0:T(2,128)(2,1)S(1)} %all_to_all.23) | data formatting | bytes 3145728
  397.3 45.4 %copy.138 = bf16[2,8,49152]{2,1,0:T(8,128)(2,1)S(1)} copy(bf16[2,8,49152]{1,0,2:T(2,128)(2,1)} %bitcast.105) | data formatting | bytes 3145728 | tf_op jit(solution)/shard_map/all_to_all | solution.py:139
  445.4 3.3 reshape.212
  448.7 3.0 multiply_reduce_fusion
  453.7 2.9 collective-permute-start.6
  456.6 2.6 collective-permute-start.5
  461.5 6.2 %collective-permute-start.7 = (bf16[16,1,34,192]{3,2,1,0:T(8,128)(2,1)S(1)}, bf16[16,1,34,192]{3,2,1,0:T(8,128)(2,1)S(1)}, u32[]{:S(2)}, u32[]{:S(2)}) collective-permute-start(bf16[16,1,34,192]{3,2,1,0:T(8,128)(2,1)S(1)} %get-tuple-element.40), channel_id=1, source_target_pairs={{0,1},{1,2},{2,3},{3,4},{4,5},{5,6},{6,7},{7,8},{8,9},{9,10},{10,1... | collective-permute-start | bytes 626696 | tf_op jit(solution)/shard_map/ppermute | solution.py:19
  469.7 6.1 fusion.5
  475.8 5.0 collective-permute-done.8
  480.8 4.9 maximum_maximum_fusion
  485.7 4.2 fusion.60
  489.9 3.7 fusion.12
  493.6 14.8 %fusion.58 = (bf16[16,8,32,192]{3,2,1,0:T(8,128)(2,1)}, bf16[16,8,32,192]{3,2,1,0:T(8,128)(2,1)}, bf16[16,8,32,192]{3,2,1,0:T(8,128)(2,1)}, bf16[16,8,32,192]{3,...) fusion(bf16[18,10,34,192]{3,2,1,0:T(8,128)(2,1)S(1)} %fusion.12), kind=kLoop, calls=%fused_computation.141 | loop fusion | bytes 56623104 | tf_op jit(solution)/shard_map/slice | solution.py:43
  508.4 7.3 %pad_maximum_fusion.12 = bf16[16,8,32,576]{3,2,1,0:T(8,128)(2,1)} fusion(bf16[16,8,32,192]{3,2,1,0:T(8,128)(2,1)} %get-tuple-element.36, bf16[16,8,32,192]{3,2,1,0:T(8,128)(2,1)} %get-tuple-element.37, bf16[16,8,32,192]{3,2,1,0:T(8,128)(2,1)} %get-tuple-element.35), kind=kLoop, calls=%fused_computation.23 | loop fusion | flops 14155776 | bytes 9437184 | tf_op jit(solution)/shard_map/concatenate | solution.py:41
  515.7 6.2 %fusion.22 = f32[4096,192]{0,1:T(8,128)} fusion(bf16[4096,576]{1,0:T(8,128)(2,1)} %bitcast.114, bf16[5184,192]{0,1:T(8,128)(2,1)} %param.18), kind=kOutput, calls=%fused_computation.72 | convolution fusion | flops 905969664 | bytes 8634368 | tf_op jit(solution)/shard_map/dot_general | solution.py:53
  521.9 6.1 pad_maximum_fusion.5
  528.0 6.1 fusion.31
  534.2 4.3 fusion.59
  538.4 4.5 pad_maximum_fusion.6
  542.9 6.0 convolution_add_fusion.6
  548.9 4.5 pad_maximum_fusion.7
  553.3 5.8 convolution_add_fusion.5
  559.1 4.5 pad_maximum_fusion.8
  563.6 5.8 convolution_add_fusion.4
  569.3 4.5 pad_maximum_fusion.9
  573.8 5.8 convolution_add_fusion.3
  579.6 4.6 pad_maximum_fusion.10
  584.2 5.8 convolution_add_fusion.2
  590.0 4.4 pad_maximum_fusion.11
  594.4 4.1 convolution_add_fusion.1
  598.5 2.9 fusion.8
  601.4 3.4 copy.141
  604.8 5.5 reshape.210
  610.3 3.3 fusion.15
  (134 shorter events, 58.0 us)
Async XLA Ops:
  2.9 18.7 %all-to-all-start = ((s32[128,1,2]{2,1,0:T(1,128)}), s32[128,1,2]{2,1,0:T(1,128)S(1)}, u32[]{:S(2)}, u32[]{:S(2)}) async-start(s32[128,1,2]{2,1,0:T(1,128)} %bitcast), calls=%async_computation | async-start | bytes 131072 | tf_op jit(solution)/shard_map/all_to_all | solution.py:116
  21.6 14.1 %all-to-all-start.1 = ((bf16[128,2,128]{2,1,0:T(2,128)(2,1)}), bf16[128,2,128]{2,1,0:T(2,128)(2,1)S(1)}, u32[]{:S(2)}, u32[]{:S(2)}) async-start(bf16[128,2,128]{2,1,0:T(2,128)(2,1)} %bitcast.2), calls=%async_computation.1 | async-start | bytes 131072 | tf_op jit(solution)/shard_map/all_to_all | solution.py:109
  36.9 7.4 %collective-permute-start.1 = (bf16[2,1,2048]{2,1,0:T(2,128)(2,1)S(1)}, bf16[2,1,2048]{2,1,0:T(2,128)(2,1)S(1)}, u32[]{:S(2)}, u32[]{:S(2)}) collective-permute-start(bf16[2,1,2048]{2,1,0:T(2,128)(2,1)S(1)} %get-tuple-element.74), channel_id=1, source_target_pairs={{1,0},{2,1},{3,2},{4,3},{5,4},{6,5},{7,6},{8,7},{9,8},{10,9},{11,1... | collective-permute-start | bytes 24584 | tf_op jit(solution)/shard_map/ppermute | solution.py:22
  39.3 5.9 collective-permute-start
  45.2 5.7 collective-permute-start.2
  56.2 6.2 %copy-start.15 = (bf16[2,4,128,16]{3,2,0,1:T(8,128)(2,1)S(1)}, bf16[2,4,128,16]{3,2,0,1:T(8,128)(2,1)}, u32[]{:S(2)}) copy-start(bf16[2,4,128,16]{3,2,0,1:T(8,128)(2,1)} %get-tuple-element.54) | copy-start | bytes 98308
  56.2 6.2 %copy-start.16 = (bf16[2,4,128,16]{3,2,0,1:T(8,128)(2,1)S(1)}, bf16[2,4,128,16]{3,2,0,1:T(8,128)(2,1)}, u32[]{:S(2)}) copy-start(bf16[2,4,128,16]{3,2,0,1:T(8,128)(2,1)} %get-tuple-element.68) | copy-start | bytes 98308
  62.3 9.5 %copy-start.14 = (bf16[2,4,128,16]{3,2,0,1:T(8,128)(2,1)S(1)}, bf16[2,4,128,16]{3,2,0,1:T(8,128)(2,1)}, u32[]{:S(2)}) copy-start(bf16[2,4,128,16]{3,2,0,1:T(8,128)(2,1)} %get-tuple-element.50) | copy-start | bytes 98308
  71.8 9.6 %copy-start.12 = (bf16[2,4,128,16]{3,2,0,1:T(8,128)(2,1)S(1)}, bf16[2,4,128,16]{3,2,0,1:T(8,128)(2,1)}, u32[]{:S(2)}) copy-start(bf16[2,4,128,16]{3,2,0,1:T(8,128)(2,1)} %get-tuple-element.71) | copy-start | bytes 98308
  71.8 9.6 %copy-start.13 = (bf16[2,4,128,16]{3,2,0,1:T(8,128)(2,1)S(1)}, bf16[2,4,128,16]{3,2,0,1:T(8,128)(2,1)}, u32[]{:S(2)}) copy-start(bf16[2,4,128,16]{3,2,0,1:T(8,128)(2,1)} %get-tuple-element.72) | copy-start | bytes 98308
  81.4 6.0 copy-start.21
  92.5 3.2 copy-start.17
  94.1 1.7 copy-start.11
  95.8 13.2 %copy-start.19 = (f32[384]{0:T(512)S(1)}, f32[384]{0:T(512)}, u32[]{:S(2)}) copy-start(f32[384]{0:T(512)} %param.14) | copy-start | bytes 4612
  100.6 10.5 %collective-permute-start.4 = (bf16[2,1,49152]{2,0,1:T(2,128)(2,1)S(1)}, bf16[2,1,49152]{2,0,1:T(2,128)(2,1)S(1)}, u32[]{:S(2)}, u32[]{:S(2)}) collective-permute-start(bf16[2,1,49152]{2,0,1:T(2,128)(2,1)S(1)} %get-tuple-element.45), channel_id=1, source_target_pairs={{1,0},{2,1},{3,2},{4,3},{5,4},{6,5},{7,6},{8,7},{9,8},{10,9},{11,1... | collective-permute-start | bytes 589832 | tf_op jit(solution)/shard_map/ppermute | solution.py:22
  102.5 10.3 %collective-permute-start.3 = (bf16[2,1,49152]{2,0,1:T(2,128)(2,1)S(1)}, bf16[2,1,49152]{2,0,1:T(2,128)(2,1)S(1)}, u32[]{:S(2)}, u32[]{:S(2)}) collective-permute-start(bf16[2,1,49152]{2,0,1:T(2,128)(2,1)S(1)} %get-tuple-element.44), channel_id=1, source_target_pairs={{0,1},{1,2},{2,3},{3,4},{4,5},{5,6},{6,7},{7,8},{8,9},{9,10},{10,1... | collective-permute-start | bytes 589832 | tf_op jit(solution)/shard_map/ppermute | solution.py:19
  233.0 9.2 %copy-start.18 = (bf16[3456,192]{0,1:T(8,128)(2,1)S(1)}, bf16[3456,192]{0,1:T(8,128)(2,1)}, u32[]{:S(2)}) copy-start(bf16[3456,192]{0,1:T(8,128)(2,1)} %param.15) | copy-start | bytes 3981316
  242.3 14.2 %slice-start = ((s8[9437184]{0:T(1024)(128)(4,1)}), s8[4194304]{0:T(1024)(128)(4,1)S(1)}, s32[]{:S(2)}) async-start(s8[9437184]{0:T(1024)(128)(4,1)} %bitcast.120), calls=%async_computation.3 | async-start | bytes 8388608
  242.3 14.2 %slice-start.1 = ((s8[9437184]{0:T(1024)(128)(4,1)}), s8[4194304]{0:T(1024)(128)(4,1)S(1)}, s32[]{:S(2)}) async-start(s8[9437184]{0:T(1024)(128)(4,1)} %bitcast.120), calls=%async_computation.4 | async-start | bytes 8388608
  249.4 7.1 %slice-start.2 = ((s8[9437184]{0:T(1024)(128)(4,1)}), s8[1048576]{0:T(1024)(128)(4,1)S(1)}, s32[]{:S(2)}) async-start(s8[9437184]{0:T(1024)(128)(4,1)} %bitcast.120), calls=%async_computation.5 | async-start | bytes 2097152
  249.4 7.1 %copy-start.23 = (f32[192]{0:T(256)S(1)}, f32[192]{0:T(256)}, u32[]{:S(2)}) copy-start(f32[192]{0:T(256)} %param.16) | copy-start | bytes 2308
  445.4 3.3 copy-start.1
  448.7 3.4 copy-start
  448.7 3.5 copy-start.22
  453.7 6.3 %collective-permute-start.6 = (bf16[16,8,1,192]{3,2,1,0:T(2,128)(2,1)S(1)}, bf16[16,8,1,192]{3,2,1,0:T(2,128)(2,1)S(1)}, u32[]{:S(2)}, u32[]{:S(2)}) collective-permute-start(bf16[16,8,1,192]{3,2,1,0:T(2,128)(2,1)S(1)} %get-tuple-element.43), channel_id=1, source_target_pairs={{16,0},{32,16},{48,32},{64,48},{80,64},{96,80},{112,96},{17,1},{33... | collective-permute-start | bytes 147464 | tf_op jit(solution)/shard_map/ppermute | solution.py:22
  456.6 4.5 collective-permute-start.5
  461.5 14.3 %collective-permute-start.7 = (bf16[16,1,34,192]{3,2,1,0:T(8,128)(2,1)S(1)}, bf16[16,1,34,192]{3,2,1,0:T(8,128)(2,1)S(1)}, u32[]{:S(2)}, u32[]{:S(2)}) collective-permute-start(bf16[16,1,34,192]{3,2,1,0:T(8,128)(2,1)S(1)} %get-tuple-element.40), channel_id=1, source_target_pairs={{0,1},{1,2},{2,3},{3,4},{4,5},{5,6},{6,7},{7,8},{8,9},{9,10},{10,1... | collective-permute-start | bytes 626696 | tf_op jit(solution)/shard_map/ppermute | solution.py:19
  467.7 13.0 %collective-permute-start.8 = (bf16[16,1,34,192]{3,2,1,0:T(8,128)(2,1)S(1)}, bf16[16,1,34,192]{3,2,1,0:T(8,128)(2,1)S(1)}, u32[]{:S(2)}, u32[]{:S(2)}) collective-permute-start(bf16[16,1,34,192]{3,2,1,0:T(8,128)(2,1)S(1)} %get-tuple-element.41), channel_id=1, source_target_pairs={{1,0},{2,1},{3,2},{4,3},{5,4},{6,5},{7,6},{8,7},{9,8},{10,9},{11,1... | collective-permute-start | bytes 626696 | tf_op jit(solution)/shard_map/ppermute | solution.py:22
  515.7 6.2 %copy-start.9 = (bf16[16,8,32,192]{3,2,1,0:T(8,128)(2,1)S(1)}, bf16[16,8,32,192]{3,2,1,0:T(8,128)(2,1)}, u32[]{:S(2)}) copy-start(bf16[16,8,32,192]{3,2,1,0:T(8,128)(2,1)} %get-tuple-element.29) | copy-start | bytes 4718596
  534.2 4.3 copy-start.8
  542.9 6.0 copy-start.7
  553.3 5.8 copy-start.6
  563.6 5.8 copy-start.5
  573.8 5.8 copy-start.4
  584.2 5.8 copy-start.10
  594.4 4.1 copy-start.3
  594.4 4.1 copy-start.20
  604.8 5.5 copy-start.2
where the time goes:
time: 624 us; the launch traced here: 614 us
  local copies, waits for them, and re-layouts  272 us (44%)
  other arithmetic  153 us (25%)
  matrix products  88.2 us (14%)
  starting transfers between devices  50.7 us (8%)
  blocking collectives  24.8 us (4%)
  waiting for transfers between devices  23.7 us (4%)
    concatenate x3, other arithmetic, upsample_conv(): jnp.concatenate([doubled[:, row_off:row_off + height, col_off:col_off + b...  75 us
    dot_general x18, matrix products, causal_taps(): jnp.dot(window.reshape(-1, 3 * channels), weight[start:start + 3 * channe...  69.6 us
    unnamed x60, local copies, waits for them, and re-layouts  64 us
    concatenate x14, other arithmetic, causal_taps(): jnp.concatenate([padded[time_off:time_off + frames, row_off:row_off + hei...  54.5 us
    another operation x2, local copies, waits for them, and re-layouts, local(): section_out.reshape(FS, 2 * TH, 2 * W * C2)  47.3 us
    all_to_all x1, local copies, waits for them, and re-layouts, local(): lax.all_to_all(section_out.reshape(FS, 2 * TH, 2 * W * C2), 'seq', split_...  45.4 us
    concatenate x3, local copies, waits for them, and re-layouts, upsample_conv(): jnp.concatenate([doubled[:, row_off:row_off + height, col_off:col_off + b...  27.4 us
    slice x6, local copies, waits for them, and re-layouts, causal_taps(): padded[time_off:time_off + frames, row_off:row_off + height, col_off:col_...  27.3 us
  transfers between devices with their start and end apart: 11, of which 8 were waited for; matrix products, arithmetic and copies ran while one was open for 2% of the time, Pallas kernels for 0%

commit v1 on v0

--- a/solution.py
+++ b/solution.py
@@ -9,6 +9,18 @@
 FS = 2
 TH = 4
 W = 128
+
+
+def split_up(shard, dim, devices):
+    shape = shard.shape
+    tiles = shard.reshape(*shape[:dim], devices, shape[dim] // devices, *shape[dim + 1 :])
+    return jnp.moveaxis(tiles, dim, 0)
+
+
+def in_order(parts, dim):
+    parts = jnp.moveaxis(parts, 0, dim)
+    shape = parts.shape
+    return parts.reshape(*shape[:dim], shape[dim] * shape[dim + 1], *shape[dim + 2 :])
 
 
 def extended_2(block, sides, width):
@@ -136,9 +148,15 @@
     act_ext = extended_2(first_act.reshape(FS, TH, W * C1), (("tile", 1),), 1)
     act_ext = jnp.pad(act_ext.reshape(FS, TH + 2, W, C1), ((0, 0), (0, 0), (1, 1), (0, 0)))
     section_out = upsample_conv(act_ext, w_up, b_up)
-    upsampled = lax.all_to_all(
-        section_out.reshape(FS, 2 * TH, 2 * W * C2), "seq", split_axis=2, concat_axis=0, tiled=True
-    )
+    value = section_out.reshape(FS, 2 * TH, 2 * W * C2)
+    devices, index = (lax.axis_size("seq"), lax.axis_index("seq"))
+    tiles = split_up(value, 2, devices)
+    done = [tiles[index]]
+    for step in range(1, devices):
+        sent = tiles[index ^ step]
+        done.append(lax.ppermute(sent, "seq", [(i_2, i_2 ^ step) for i_2 in range(devices)]))
+    tiles = jnp.stack(done)[index ^ jnp.arange(devices)]
+    upsampled = in_order(tiles, 0)
     upsampled = upsampled.reshape(FS * seq_count, 2 * TH, 2 * W // seq_count, C2)
     res_act = normed_silu(upsampled.astype(jnp.float32), gain_res)
     res_ext = extended_2(res_act, (("seq", 2), ("tile", 1)), 1)

time: 624 us -> 470 us (0.75)
  local copies, waits for them, and re-layouts: 272 us -> 124 us
  blocking collectives: 24.8 us -> 0 us
  waiting for transfers between devices: 23.7 us -> 40.2 us
  starting transfers between devices: 50.7 us -> 60.1 us
    unnamed x60 -> x71, local copies, waits for them, and re-layouts: 64 us -> 2.94 us
    all_to_all x1 -> x0, local copies, waits for them, and re-layouts: 45.4 us -> none  [local(): lax.all_to_all(section_out.reshape(FS, 2 * TH, 2 * W * C2), 'seq', split_...]
    another operation x2 -> x3, local copies, waits for them, and re-layouts: 47.3 us -> 7.09 us  [the longest x1 3.66 us: split_up(): shard.reshape(*shape[:dim], devices, shape[dim] // devices, *shape[dim +...]
    all_to_all x1 -> x0, blocking collectives: 24.8 us -> none  [local(): lax.all_to_all(section_out.reshape(FS, 2 * TH, 2 * W * C2), 'seq', split_...]
    ppermute x0 -> x7, waiting for transfers between devices: none -> 17 us  [local(): lax.ppermute(sent, 'seq', [(i_2, i_2 ^ step) for i_2 in range(devices)])]
    ppermute x0 -> x7, starting transfers between devices: none -> 9.32 us  [local(): lax.ppermute(sent, 'seq', [(i_2, i_2 ^ step) for i_2 in range(devices)])]
  transfers between devices with their start and end apart: 11 -> 18, of which waited for: 8 -> 13; matrix products, arithmetic and copies ran while one was open for 2% -> 3% of each run, Pallas kernels for 0% -> 0%
where the time goes in v1:
time: 470 us; the launch traced here: 465 us
  other arithmetic  153 us (33%)
  local copies, waits for them, and re-layouts  124 us (26%)
  matrix products  86.7 us (18%)
  starting transfers between devices  60.1 us (13%)
  waiting for transfers between devices  40.2 us (9%)
    concatenate x3, other arithmetic, upsample_conv(): jnp.concatenate([doubled[:, row_off:row_off + height, col_off:col_off + b...  74.8 us
    dot_general x18, matrix products, causal_taps(): jnp.dot(window.reshape(-1, 3 * channels), weight[start:start + 3 * channe...  69.2 us
    concatenate x14, other arithmetic, causal_taps(): jnp.concatenate([padded[time_off:time_off + frames, row_off:row_off + hei...  54.1 us
    concatenate x3, local copies, waits for them, and re-layouts, upsample_conv(): jnp.concatenate([doubled[:, row_off:row_off + height, col_off:col_off + b...  27.5 us
    slice x6, local copies, waits for them, and re-layouts, causal_taps(): padded[time_off:time_off + frames, row_off:row_off + height, col_off:col_...  27.3 us
    ppermute x4, starting transfers between devices, extended_2(): lax.ppermute(lax.slice_in_dim(block, block.shape[dim] - width, None, axis...  21.3 us
    slice x1, local copies, waits for them, and re-layouts, upsample_conv(): doubled[:, row_off:row_off + height, col_off:col_off + breadth]  20.8 us
    dot_general x3, matrix products, upsample_conv(): jnp.dot(window.reshape(-1, 3 * channels), weight[start:start + 3 * channe...  17.4 us
  transfers between devices with their start and end apart: 18, of which 13 were waited for; matrix products, arithmetic and copies ran while one was open for 3% of the time, Pallas kernels for 0%

profile of v1, /device:TPU:7, one launch (start us, length us, event | category | flops | bytes accessed | tf_op | source)
XLA Modules:
  0.0 465.2 jit_solution(6305916066521335721)
XLA Ops:
  2.9 10.8 %all-to-all-start = ((s32[128,1,2]{2,1,0:T(1,128)}), s32[128,1,2]{2,1,0:T(1,128)S(1)}, u32[]{:S(2)}, u32[]{:S(2)}) async-start(s32[128,1,2]{2,1,0:T(1,128)} %bitcast), calls=%async_computation | async-start | bytes 131072 | tf_op jit(solution)/shard_map/all_to_all | solution.py:128
  15.4 6.2 %all-to-all-done = s32[128,1,2]{2,1,0:T(1,128)S(1)} async-done(((s32[128,1,2]{2,1,0:T(1,128)}), s32[128,1,2]{2,1,0:T(1,128)S(1)}, u32[]{:S(2)}, u32[]{:S(2)}) %all-to-all-start) | async-done | bytes 1056 | tf_op jit(solution)/shard_map/all_to_all | solution.py:128
  21.6 6.1 %all-to-all-start.1 = ((bf16[128,2,128]{2,1,0:T(2,128)(2,1)}), bf16[128,2,128]{2,1,0:T(2,128)(2,1)S(1)}, u32[]{:S(2)}, u32[]{:S(2)}) async-start(bf16[128,2,128]{2,1,0:T(2,128)(2,1)} %bitcast.2), calls=%async_computation.1 | async-start | bytes 131072 | tf_op jit(solution)/shard_map/all_to_all | solution.py:121
  29.1 6.5 %all-to-all-done.1 = bf16[128,2,128]{2,1,0:T(2,128)(2,1)S(1)} async-done(((bf16[128,2,128]{2,1,0:T(2,128)(2,1)}), bf16[128,2,128]{2,1,0:T(2,128)(2,1)S(1)}, u32[]{:S(2)}, u32[]{:S(2)}) %all-to-all-start.1) | async-done | bytes 65568 | tf_op jit(solution)/shard_map/all_to_all | solution.py:121
  36.9 2.4 collective-permute-start.1
  39.3 5.0 %collective-permute-start = (bf16[2,1,2048]{2,1,0:T(2,128)(2,1)S(1)}, bf16[2,1,2048]{2,1,0:T(2,128)(2,1)S(1)}, u32[]{:S(2)}, u32[]{:S(2)}) collective-permute-start(bf16[2,1,2048]{2,1,0:T(2,128)(2,1)S(1)} %get-tuple-element.81), channel_id=1, source_target_pairs={{0,1},{1,2},{2,3},{3,4},{4,5},{5,6},{6,7},{7,8},{8,9},{9,10},{10,1... | collective-permute-start | bytes 24584 | tf_op jit(solution)/shard_map/ppermute | solution.py:31
  45.2 4.3 collective-permute-start.2
  62.5 2.5 pad_maximum_fusion.22
  66.2 2.3 fusion.39
  69.7 2.3 fusion.41
  72.0 2.6 pad_maximum_fusion.20
  79.2 2.3 fusion.45
  83.9 2.4 fusion.49
  87.7 4.8 %multiply_reduce_fusion.1 = (f32[1024]{0:T(1024)S(1)}, f32[1024,384]{1,0:T(8,128)S(1)}) fusion(f32[384]{0:T(512)S(1)} %copy-done.21, bf16[1024,48]{0,1:T(8,128)(2,1)S(1)} %reshape.218, bf16[432,384]{1,0:T(8,128)(2,1)} %param.12, f32[1024,384]{1,0:T(8,128)S(1)} %fusion.35, f32[1024,384]{1,0:T(8,128)} %fusion.37, f32[1024,384]{1,0:T(8,128)} %fusion.39, ...), kind=kOutput, calls=%fused_computation.52 | convolution fusion | flops 42073088 | bytes 14296576 | tf_op jit(solution)/shard_map/dot_general | solution.py:65
  96.0 4.5 fusion.17
  102.7 6.5 %collective-permute-start.3 = (bf16[2,1,49152]{2,0,1:T(2,128)(2,1)S(1)}, bf16[2,1,49152]{2,0,1:T(2,128)(2,1)S(1)}, u32[]{:S(2)}, u32[]{:S(2)}) collective-permute-start(bf16[2,1,49152]{2,0,1:T(2,128)(2,1)S(1)} %get-tuple-element.52), channel_id=1, source_target_pairs={{0,1},{1,2},{2,3},{3,4},{4,5},{5,6},{6,7},{7,8},{8,9},{9,10},{10,1... | collective-permute-start | bytes 589832 | tf_op jit(solution)/shard_map/ppermute | solution.py:31
  116.7 2.7 broadcast_in_dim.14
  119.3 20.8 %fusion.58 = (bf16[2,8,256,384]{3,0,2,1:T(2,128)(2,1)S(1)}, bf16[2,8,256,384]{3,0,2,1:T(2,128)(2,1)}, bf16[2,8,256,384]{3,0,2,1:T(2,128)(2,1)}, bf16[2,8,256,384...) fusion(bf16[2,12,260,384]{3,0,2,1:T(2,128)(2,1)S(1)} %bitcast.130), kind=kLoop, calls=%fused_computation.166 | loop fusion | bytes 56623104 | tf_op jit(solution)/shard_map/slice | solution.py:83
  140.1 30.7 %pad_maximum_fusion = bf16[2,8,256,1152]{3,0,2,1:T(2,128)(2,1)} fusion(bf16[2,8,256,384]{3,0,2,1:T(2,128)(2,1)S(1)} %get-tuple-element.11, bf16[2,8,256,384]{3,0,2,1:T(2,128)(2,1)S(1)} %get-tuple-element.12, bf16[2,8,256,384]{3,0,2,1:T(2,128)(2,1)S(1)} %get-tuple-element.13), kind=kLoop, calls=%fused_computation.4 | loop fusion | flops 28311552 | bytes 18874368 | tf_op jit(solution)/shard_map/concatenate | solution.py:81
  170.8 9.1 %copy.102 = bf16[2,8,256,1152]{3,2,1,0:T(8,128)(2,1)} copy(bf16[2,8,256,1152]{3,0,2,1:T(2,128)(2,1)} %pad_maximum_fusion) | data formatting | bytes 18874368 | tf_op jit(solution)/shard_map/concatenate | solution.py:81
  179.9 13.0 %pad_maximum_fusion.1 = bf16[2,8,256,1152]{3,0,2,1:T(2,128)(2,1)} fusion(bf16[2,8,256,384]{3,0,2,1:T(2,128)(2,1)} %get-tuple-element.8, bf16[2,8,256,384]{3,0,2,1:T(2,128)(2,1)} %get-tuple-element.9, bf16[2,8,256,384]{3,0,2,1:T(2,128)(2,1)} %get-tuple-element.10), kind=kLoop, calls=%fused_computation.5 | loop fusion | flops 28311552 | bytes 18874368 | tf_op jit(solution)/shard_map/concatenate | solution.py:81
  192.9 9.1 %copy.103 = bf16[2,8,256,1152]{3,2,1,0:T(8,128)(2,1)} copy(bf16[2,8,256,1152]{3,0,2,1:T(2,128)(2,1)} %pad_maximum_fusion.1) | data formatting | bytes 18874368 | tf_op jit(solution)/shard_map/concatenate | solution.py:81
  202.1 31.1 %pad_maximum_fusion.2 = bf16[2,8,256,1152]{3,0,2,1:T(2,128)(2,1)} fusion(bf16[2,8,256,384]{3,0,2,1:T(2,128)(2,1)} %get-tuple-element.6, bf16[2,8,256,384]{3,0,2,1:T(2,128)(2,1)} %get-tuple-element.7, bf16[2,8,256,384]{3,0,2,1:T(2,128)(2,1)S(1)} %get-tuple-element.5), kind=kLoop, calls=%fused_computation.6 | loop fusion | flops 28311552 | bytes 18874368 | tf_op jit(solution)/shard_map/concatenate | solution.py:81
  233.2 9.2 %copy.104 = bf16[2,8,256,1152]{3,2,1,0:T(8,128)(2,1)} copy(bf16[2,8,256,1152]{3,0,2,1:T(2,128)(2,1)} %pad_maximum_fusion.2) | data formatting | bytes 18874368 | tf_op jit(solution)/shard_map/concatenate | solution.py:81
  242.4 7.1 %fusion.20 = f32[4096,192]{0,1:T(8,128)S(1)} fusion(bf16[4096,1152]{1,0:T(8,128)(2,1)} %bitcast.143, bf16[3456,192]{0,1:T(8,128)(2,1)S(1)} %copy-done.18), kind=kOutput, calls=%fused_computation.58 | convolution fusion | flops 1811939328 | bytes 13025280 | tf_op jit(solution)/shard_map/dot_general | solution.py:89
  249.6 7.1 %convolution_add_fusion.8 = f32[4096,192]{0,1:T(8,128)S(1)} fusion(f32[4096,192]{0,1:T(8,128)S(1)} %fusion.20, bf16[4096,1152]{1,0:T(8,128)(2,1)} %bitcast.131, bf16[3456,192]{0,1:T(8,128)(2,1)S(1)} %copy-done.18), kind=kOutput, calls=%fused_computation.36 | convolution fusion | flops 1812725760 | bytes 16171008 | tf_op jit(solution)/shard_map/dot_general | solution.py:89
  256.7 3.3 fusion.10
  260.0 2.5 copy.105
  262.5 3.7 reshape_reshape_reshape.3
  266.2 3.4 constant_dynamic-slice_fusion
  282.2 4.3 collective-permute-done.8
  286.5 4.4 collective-permute-done.9
  292.2 4.8 %collective-permute-done.11 = bf16[2,8,6144]{2,1,0:T(8,128)(2,1)S(1)} collective-permute-done((bf16[2,8,6144]{2,1,0:T(8,128)(2,1)S(1)}, bf16[2,8,6144]{2,1,0:T(8,128)(2,1)S(1)}, u32[]{:S(2)}, u32[]{:S(2)}) %collective-permute-start.11) | collective-permute-done | bytes 196640 | tf_op jit(solution)/shard_map/ppermute | solution.py:157
  297.7 3.5 reshape.237
  301.2 3.0 multiply_reduce_fusion
  308.1 3.6 collective-permute-start.12
  314.0 6.2 %collective-permute-start.14 = (bf16[16,1,34,192]{3,2,1,0:T(8,128)(2,1)S(1)}, bf16[16,1,34,192]{3,2,1,0:T(8,128)(2,1)S(1)}, u32[]{:S(2)}, u32[]{:S(2)}) collective-permute-start(bf16[16,1,34,192]{3,2,1,0:T(8,128)(2,1)S(1)} %get-tuple-element.40), channel_id=1, source_target_pairs={{0,1},{1,2},{2,3},{3,4},{4,5},{5,6},{6,7},{7,8},{8,9},{9,10},{10,1... | collective-permute-start | bytes 626696 | tf_op jit(solution)/shard_map/ppermute | solution.py:31
  322.2 5.7 %fusion.5 = bf16[16,8,32,576]{3,2,1,0:T(8,128)(2,1)S(1)} fusion(bf16[16,8,1,192]{3,2,1,0:T(2,128)(2,1)S(1)} %collective-permute-done.13, bf16[16,8,32,192]{3,2,1,0:T(8,128)(2,1)S(1)} %multiply_convert_fusion, bf16[16,8,1,192]{3,2,1,0:T(2,128)(2,1)S(1)} %collective-permute-done.12), kind=kLoop, calls=%fused_computation.14 | loop fusion | flops 23592960 | bytes 6389760 | tf_op jit(solution)/shard_map/concatenate | solution.py:53
  327.9 4.4 collective-permute-done.15
  332.3 4.9 %maximum_maximum_fusion = (bf16[16,9,34,192]{3,2,1,0:T(8,128)(2,1)S(1)}, bf16[16,9,34,192]{3,2,1,0:T(8,128)(2,1)S(1)}) fusion(bf16[16,8,1,192]{3,2,1,0:T(2,128)(2,1)S(1)} %collective-permute-done.13, bf16[16,8,32,192]{3,2,1,0:T(8,128)(2,1)S(1)} %multiply_convert_fusion, bf16[16,8,1,192]{3,2,1,0:T(2,128)(2,1)S(1)} %collective-permute-done.12, ...), kind=kLoop, calls=%fused_computation.46 | loop fusion | flops 15040512 | bytes 5849088 | tf_op jit(solution)/shard_map/concatenate | solution.py:35
  337.3 4.2 fusion.61
  341.5 3.7 fusion.12
  345.2 14.7 %fusion.59 = (bf16[16,8,32,192]{3,2,1,0:T(8,128)(2,1)}, bf16[16,8,32,192]{3,2,1,0:T(8,128)(2,1)}, bf16[16,8,32,192]{3,2,1,0:T(8,128)(2,1)}, bf16[16,8,32,192]{3,...) fusion(bf16[18,10,34,192]{3,2,1,0:T(8,128)(2,1)S(1)} %fusion.12), kind=kLoop, calls=%fused_computation.167 | loop fusion | bytes 56623104 | tf_op jit(solution)/shard_map/slice | solution.py:55
  359.9 7.3 %pad_maximum_fusion.12 = bf16[16,8,32,576]{3,2,1,0:T(8,128)(2,1)} fusion(bf16[16,8,32,192]{3,2,1,0:T(8,128)(2,1)} %get-tuple-element.36, bf16[16,8,32,192]{3,2,1,0:T(8,128)(2,1)} %get-tuple-element.37, bf16[16,8,32,192]{3,2,1,0:T(8,128)(2,1)} %get-tuple-element.35), kind=kLoop, calls=%fused_computation.24 | loop fusion | flops 14155776 | bytes 9437184 | tf_op jit(solution)/shard_map/concatenate | solution.py:53
  367.3 6.3 %fusion.22 = f32[4096,192]{0,1:T(8,128)} fusion(bf16[4096,576]{1,0:T(8,128)(2,1)} %bitcast.139, bf16[5184,192]{0,1:T(8,128)(2,1)} %param.18), kind=kOutput, calls=%fused_computation.72 | convolution fusion | flops 905969664 | bytes 8634368 | tf_op jit(solution)/shard_map/dot_general | solution.py:65
  373.5 6.2 %pad_maximum_fusion.5 = bf16[16,8,32,576]{3,2,1,0:T(8,128)(2,1)} fusion(bf16[16,8,32,192]{3,2,1,0:T(8,128)(2,1)S(1)} %get-tuple-element.28, bf16[16,8,32,192]{3,2,1,0:T(8,128)(2,1)S(1)} %copy-done.9, bf16[16,8,32,192]{3,2,1,0:T(8,128)(2,1)} %get-tuple-element.30), kind=kLoop, calls=%fused_computation.17 | loop fusion | flops 14155776 | bytes 9437184 | tf_op jit(solution)/shard_map/concatenate | solution.py:53
  379.7 6.0 %fusion.31 = f32[4096,192]{0,1:T(8,128)} fusion(bf16[4096,576]{1,0:T(8,128)(2,1)} %bitcast.140, bf16[5184,192]{0,1:T(8,128)(2,1)} %param.18), kind=kOutput, calls=%fused_computation.81 | convolution fusion | flops 905969664 | bytes 8634368 | tf_op jit(solution)/shard_map/dot_general | solution.py:65
  385.7 4.2 fusion.60
  389.9 4.5 pad_maximum_fusion.6
  394.4 5.9 %convolution_add_fusion.6 = f32[4096,192]{0,1:T(8,128)} fusion(f32[4096,192]{0,1:T(8,128)} %fusion.31, bf16[4096,576]{1,0:T(8,128)(2,1)S(1)} %bitcast.133, bf16[5184,192]{0,1:T(8,128)(2,1)} %param.18), kind=kOutput, calls=%fused_computation.31 | convolution fusion | flops 906756096 | bytes 11255808 | tf_op jit(solution)/shard_map/dot_general | solution.py:65
  400.3 4.5 pad_maximum_fusion.7
  404.8 5.7 %convolution_add_fusion.5 = f32[4096,192]{0,1:T(8,128)} fusion(f32[4096,192]{0,1:T(8,128)} %convolution_add_fusion.6, bf16[4096,576]{1,0:T(8,128)(2,1)S(1)} %bitcast.134, bf16[5184,192]{0,1:T(8,128)(2,1)} %param.18), kind=kOutput, calls=%fused_computation.30 | convolution fusion | flops 906756096 | bytes 11255808 | tf_op jit(solution)/shard_map/dot_general | solution.py:65
  410.5 4.5 pad_maximum_fusion.8
  415.0 5.7 %convolution_add_fusion.4 = f32[4096,192]{0,1:T(8,128)} fusion(f32[4096,192]{0,1:T(8,128)} %convolution_add_fusion.5, bf16[4096,576]{1,0:T(8,128)(2,1)S(1)} %bitcast.135, bf16[5184,192]{0,1:T(8,128)(2,1)} %param.18), kind=kOutput, calls=%fused_computation.29 | convolution fusion | flops 906756096 | bytes 11255808 | tf_op jit(solution)/shard_map/dot_general | solution.py:65
  420.7 4.5 pad_maximum_fusion.9
  425.1 5.7 %convolution_add_fusion.3 = f32[4096,192]{0,1:T(8,128)} fusion(f32[4096,192]{0,1:T(8,128)} %convolution_add_fusion.4, bf16[4096,576]{1,0:T(8,128)(2,1)S(1)} %bitcast.136, bf16[5184,192]{0,1:T(8,128)(2,1)} %param.18), kind=kOutput, calls=%fused_computation.28 | convolution fusion | flops 906756096 | bytes 11255808 | tf_op jit(solution)/shard_map/dot_general | solution.py:65
  430.8 4.6 pad_maximum_fusion.10
  435.5 5.7 %convolution_add_fusion.2 = f32[4096,192]{0,1:T(8,128)} fusion(f32[4096,192]{0,1:T(8,128)} %convolution_add_fusion.3, bf16[4096,576]{1,0:T(8,128)(2,1)S(1)} %bitcast.137, bf16[5184,192]{0,1:T(8,128)(2,1)} %param.18), kind=kOutput, calls=%fused_computation.27 | convolution fusion | flops 906756096 | bytes 11255808 | tf_op jit(solution)/shard_map/dot_general | solution.py:65
  441.2 4.4 pad_maximum_fusion.11
  445.6 4.1 convolution_add_fusion.1
  449.7 2.9 fusion.8
  452.6 3.3 copy.106
  455.9 5.5 %reshape.235 = f32[16,8,6144]{2,1,0:T(8,128)} reshape(f32[4096,192]{1,0:T(8,128)} %copy.106) | data formatting | bytes 6291456 | tf_op jit(solution)/shard_map/reshape | solution.py:70
  461.4 3.3 fusion.15
  (160 shorter events, 67.3 us)
Async XLA Ops:
  2.9 18.7 %all-to-all-start = ((s32[128,1,2]{2,1,0:T(1,128)}), s32[128,1,2]{2,1,0:T(1,128)S(1)}, u32[]{:S(2)}, u32[]{:S(2)}) async-start(s32[128,1,2]{2,1,0:T(1,128)} %bitcast), calls=%async_computation | async-start | bytes 131072 | tf_op jit(solution)/shard_map/all_to_all | solution.py:128
  21.6 14.1 %all-to-all-start.1 = ((bf16[128,2,128]{2,1,0:T(2,128)(2,1)}), bf16[128,2,128]{2,1,0:T(2,128)(2,1)S(1)}, u32[]{:S(2)}, u32[]{:S(2)}) async-start(bf16[128,2,128]{2,1,0:T(2,128)(2,1)} %bitcast.2), calls=%async_computation.1 | async-start | bytes 131072 | tf_op jit(solution)/shard_map/all_to_all | solution.py:121
  36.9 7.4 %collective-permute-start.1 = (bf16[2,1,2048]{2,1,0:T(2,128)(2,1)S(1)}, bf16[2,1,2048]{2,1,0:T(2,128)(2,1)S(1)}, u32[]{:S(2)}, u32[]{:S(2)}) collective-permute-start(bf16[2,1,2048]{2,1,0:T(2,128)(2,1)S(1)} %get-tuple-element.82), channel_id=1, source_target_pairs={{1,0},{2,1},{3,2},{4,3},{5,4},{6,5},{7,6},{8,7},{9,8},{10,9},{11,1... | collective-permute-start | bytes 24584 | tf_op jit(solution)/shard_map/ppermute | solution.py:34
  39.3 5.8 %collective-permute-start = (bf16[2,1,2048]{2,1,0:T(2,128)(2,1)S(1)}, bf16[2,1,2048]{2,1,0:T(2,128)(2,1)S(1)}, u32[]{:S(2)}, u32[]{:S(2)}) collective-permute-start(bf16[2,1,2048]{2,1,0:T(2,128)(2,1)S(1)} %get-tuple-element.81), channel_id=1, source_target_pairs={{0,1},{1,2},{2,3},{3,4},{4,5},{5,6},{6,7},{7,8},{8,9},{9,10},{10,1... | collective-permute-start | bytes 24584 | tf_op jit(solution)/shard_map/ppermute | solution.py:31
  45.2 5.8 %collective-permute-start.2 = (bf16[2,6,2048]{2,1,0:T(8,128)(2,1)S(1)}, bf16[2,6,2048]{2,1,0:T(8,128)(2,1)S(1)}, u32[]{:S(2)}, u32[]{:S(2)}) collective-permute-start(bf16[2,6,2048]{2,1,0:T(8,128)(2,1)S(1)} %pad_maximum_fusion.27), channel_id=1, source_target_pairs={{0,16},{16,32},{32,48},{48,64},{64,80},{80,96},{96,112},{1,17},{17... | collective-permute-start | bytes 147464 | tf_op jit(solution)/shard_map/ppermute | solution.py:42
  56.3 6.2 %copy-start.15 = (bf16[2,4,128,16]{3,2,0,1:T(8,128)(2,1)S(1)}, bf16[2,4,128,16]{3,2,0,1:T(8,128)(2,1)}, u32[]{:S(2)}) copy-start(bf16[2,4,128,16]{3,2,0,1:T(8,128)(2,1)} %get-tuple-element.62) | copy-start | bytes 98308
  56.3 6.2 %copy-start.16 = (bf16[2,4,128,16]{3,2,0,1:T(8,128)(2,1)S(1)}, bf16[2,4,128,16]{3,2,0,1:T(8,128)(2,1)}, u32[]{:S(2)}) copy-start(bf16[2,4,128,16]{3,2,0,1:T(8,128)(2,1)} %get-tuple-element.76) | copy-start | bytes 98308
  62.5 9.5 %copy-start.14 = (bf16[2,4,128,16]{3,2,0,1:T(8,128)(2,1)S(1)}, bf16[2,4,128,16]{3,2,0,1:T(8,128)(2,1)}, u32[]{:S(2)}) copy-start(bf16[2,4,128,16]{3,2,0,1:T(8,128)(2,1)} %get-tuple-element.58) | copy-start | bytes 98308
  72.0 9.6 %copy-start.12 = (bf16[2,4,128,16]{3,2,0,1:T(8,128)(2,1)S(1)}, bf16[2,4,128,16]{3,2,0,1:T(8,128)(2,1)}, u32[]{:S(2)}) copy-start(bf16[2,4,128,16]{3,2,0,1:T(8,128)(2,1)} %get-tuple-element.79) | copy-start | bytes 98308
  72.0 9.6 %copy-start.13 = (bf16[2,4,128,16]{3,2,0,1:T(8,128)(2,1)S(1)}, bf16[2,4,128,16]{3,2,0,1:T(8,128)(2,1)}, u32[]{:S(2)}) copy-start(bf16[2,4,128,16]{3,2,0,1:T(8,128)(2,1)} %get-tuple-element.80) | copy-start | bytes 98308
  81.6 6.1 %copy-start.21 = (f32[384]{0:T(512)S(1)}, f32[384]{0:T(512)}, u32[]{:S(2)}) copy-start(f32[384]{0:T(512)} %param.13) | copy-start | bytes 4612
  92.7 3.2 copy-start.17
  94.3 1.7 copy-start.11
  96.0 13.2 %copy-start.19 = (f32[384]{0:T(512)S(1)}, f32[384]{0:T(512)}, u32[]{:S(2)}) copy-start(f32[384]{0:T(512)} %param.14) | copy-start | bytes 4612
  100.8 10.5 %collective-permute-start.4 = (bf16[2,1,49152]{2,0,1:T(2,128)(2,1)S(1)}, bf16[2,1,49152]{2,0,1:T(2,128)(2,1)S(1)}, u32[]{:S(2)}, u32[]{:S(2)}) collective-permute-start(bf16[2,1,49152]{2,0,1:T(2,128)(2,1)S(1)} %get-tuple-element.53), channel_id=1, source_target_pairs={{1,0},{2,1},{3,2},{4,3},{5,4},{6,5},{7,6},{8,7},{9,8},{10,9},{11,1... | collective-permute-start | bytes 589832 | tf_op jit(solution)/shard_map/ppermute | solution.py:34
  102.7 10.4 %collective-permute-start.3 = (bf16[2,1,49152]{2,0,1:T(2,128)(2,1)S(1)}, bf16[2,1,49152]{2,0,1:T(2,128)(2,1)S(1)}, u32[]{:S(2)}, u32[]{:S(2)}) collective-permute-start(bf16[2,1,49152]{2,0,1:T(2,128)(2,1)S(1)} %get-tuple-element.52), channel_id=1, source_target_pairs={{0,1},{1,2},{2,3},{3,4},{4,5},{5,6},{6,7},{7,8},{8,9},{9,10},{10,1... | collective-permute-start | bytes 589832 | tf_op jit(solution)/shard_map/ppermute | solution.py:31
  233.2 9.2 %copy-start.18 = (bf16[3456,192]{0,1:T(8,128)(2,1)S(1)}, bf16[3456,192]{0,1:T(8,128)(2,1)}, u32[]{:S(2)}) copy-start(bf16[3456,192]{0,1:T(8,128)(2,1)} %param.15) | copy-start | bytes 3981316
  242.4 14.2 %slice-start = ((s8[9437184]{0:T(1024)(128)(4,1)}), s8[4194304]{0:T(1024)(128)(4,1)S(1)}, s32[]{:S(2)}) async-start(s8[9437184]{0:T(1024)(128)(4,1)} %bitcast.144), calls=%async_computation.2 | async-start | bytes 8388608
  242.4 14.2 %slice-start.1 = ((s8[9437184]{0:T(1024)(128)(4,1)}), s8[4194304]{0:T(1024)(128)(4,1)S(1)}, s32[]{:S(2)}) async-start(s8[9437184]{0:T(1024)(128)(4,1)} %bitcast.144), calls=%async_computation.3 | async-start | bytes 8388608
  249.5 7.1 %slice-start.2 = ((s8[9437184]{0:T(1024)(128)(4,1)}), s8[1048576]{0:T(1024)(128)(4,1)S(1)}, s32[]{:S(2)}) async-start(s8[9437184]{0:T(1024)(128)(4,1)} %bitcast.144), calls=%async_computation.4 | async-start | bytes 2097152
  249.6 7.1 %copy-start.23 = (f32[192]{0:T(256)S(1)}, f32[192]{0:T(256)}, u32[]{:S(2)}) copy-start(f32[192]{0:T(256)} %param.16) | copy-start | bytes 2308
  269.7 6.7 %collective-permute-start.5 = (bf16[2,8,6144]{2,1,0:T(8,128)(2,1)S(1)}, bf16[2,8,6144]{2,1,0:T(8,128)(2,1)S(1)}, u32[]{:S(2)}, u32[]{:S(2)}) collective-permute-start(bf16[2,8,6144]{2,1,0:T(8,128)(2,1)S(1)} %bitcast.157), channel_id=1, source_target_pairs={{0,16},{16,0},{32,48},{48,32},{64,80},{80,64},{96,112},{112,96},{1... | collective-permute-start | bytes 589832 | tf_op jit(solution)/shard_map/ppermute | solution.py:157
  270.1 8.0 %collective-permute-start.6 = (bf16[2,8,6144]{2,1,0:T(8,128)(2,1)S(1)}, bf16[2,8,6144]{2,1,0:T(8,128)(2,1)S(1)}, u32[]{:S(2)}, u32[]{:S(2)}) collective-permute-start(bf16[2,8,6144]{2,1,0:T(8,128)(2,1)S(1)} %bitcast.156), channel_id=1, source_target_pairs={{0,32},{16,48},{32,0},{48,16},{64,96},{80,112},{96,64},{112,80},{1... | collective-permute-start | bytes 589832 | tf_op jit(solution)/shard_map/ppermute | solution.py:157
  271.5 10.7 %collective-permute-start.7 = (bf16[2,8,6144]{2,1,0:T(8,128)(2,1)S(1)}, bf16[2,8,6144]{2,1,0:T(8,128)(2,1)S(1)}, u32[]{:S(2)}, u32[]{:S(2)}) collective-permute-start(bf16[2,8,6144]{2,1,0:T(8,128)(2,1)S(1)} %bitcast.155), channel_id=1, source_target_pairs={{0,48},{16,32},{32,16},{48,0},{64,112},{80,96},{96,80},{112,64},{1... | collective-permute-start | bytes 589832 | tf_op jit(solution)/shard_map/ppermute | solution.py:157
  272.6 13.9 %collective-permute-start.8 = (bf16[2,8,6144]{2,1,0:T(8,128)(2,1)S(1)}, bf16[2,8,6144]{2,1,0:T(8,128)(2,1)S(1)}, u32[]{:S(2)}, u32[]{:S(2)}) collective-permute-start(bf16[2,8,6144]{2,1,0:T(8,128)(2,1)S(1)} %bitcast.154), channel_id=1, source_target_pairs={{0,64},{16,80},{32,96},{48,112},{64,0},{80,16},{96,32},{112,48},{1... | collective-permute-start | bytes 589832 | tf_op jit(solution)/shard_map/ppermute | solution.py:157
  274.7 16.2 %collective-permute-start.9 = (bf16[2,8,6144]{2,1,0:T(8,128)(2,1)S(1)}, bf16[2,8,6144]{2,1,0:T(8,128)(2,1)S(1)}, u32[]{:S(2)}, u32[]{:S(2)}) collective-permute-start(bf16[2,8,6144]{2,1,0:T(8,128)(2,1)S(1)} %bitcast.153), channel_id=1, source_target_pairs={{0,80},{16,64},{32,112},{48,96},{64,16},{80,0},{96,48},{112,32},{1... | collective-permute-start | bytes 589832 | tf_op jit(solution)/shard_map/ppermute | solution.py:157
  276.5 15.8 %collective-permute-start.10 = (bf16[2,8,6144]{2,1,0:T(8,128)(2,1)S(1)}, bf16[2,8,6144]{2,1,0:T(8,128)(2,1)S(1)}, u32[]{:S(2)}, u32[]{:S(2)}) collective-permute-start(bf16[2,8,6144]{2,1,0:T(8,128)(2,1)S(1)} %bitcast.152), channel_id=1, source_target_pairs={{0,96},{16,112},{32,64},{48,80},{64,32},{80,48},{96,0},{112,16},{1... | collective-permute-start | bytes 589832 | tf_op jit(solution)/shard_map/ppermute | solution.py:157
  278.2 18.9 %collective-permute-start.11 = (bf16[2,8,6144]{2,1,0:T(8,128)(2,1)S(1)}, bf16[2,8,6144]{2,1,0:T(8,128)(2,1)S(1)}, u32[]{:S(2)}, u32[]{:S(2)}) collective-permute-start(bf16[2,8,6144]{2,1,0:T(8,128)(2,1)S(1)} %bitcast.151), channel_id=1, source_target_pairs={{0,112},{16,96},{32,80},{48,64},{64,48},{80,32},{96,16},{112,0},{1... | collective-permute-start | bytes 589832 | tf_op jit(solution)/shard_map/ppermute | solution.py:157
  297.7 6.5 %copy-start.2 = (bf16[8,2,8,6144]{3,2,1,0:T(8,128)(2,1)}, bf16[8,2,8,6144]{3,2,1,0:T(8,128)(2,1)S(1)}, u32[]{:S(2)}) copy-start(bf16[8,2,8,6144]{3,2,1,0:T(8,128)(2,1)S(1)} %gather_fusion) | copy-start | bytes 4718596
  301.2 3.4 copy-start
  301.2 3.4 copy-start.22
  306.2 6.3 %collective-permute-start.13 = (bf16[16,8,1,192]{3,2,1,0:T(2,128)(2,1)S(1)}, bf16[16,8,1,192]{3,2,1,0:T(2,128)(2,1)S(1)}, u32[]{:S(2)}, u32[]{:S(2)}) collective-permute-start(bf16[16,8,1,192]{3,2,1,0:T(2,128)(2,1)S(1)} %get-tuple-element.43), channel_id=1, source_target_pairs={{16,0},{32,16},{48,32},{64,48},{80,64},{96,80},{112,96},{17,1},{33... | collective-permute-start | bytes 147464 | tf_op jit(solution)/shard_map/ppermute | solution.py:34
  308.1 5.6 %collective-permute-start.12 = (bf16[16,8,1,192]{3,2,1,0:T(2,128)(2,1)S(1)}, bf16[16,8,1,192]{3,2,1,0:T(2,128)(2,1)S(1)}, u32[]{:S(2)}, u32[]{:S(2)}) collective-permute-start(bf16[16,8,1,192]{3,2,1,0:T(2,128)(2,1)S(1)} %get-tuple-element.42), channel_id=1, source_target_pairs={{0,16},{16,32},{32,48},{48,64},{64,80},{80,96},{96,112},{1,17},{17... | collective-permute-start | bytes 147464 | tf_op jit(solution)/shard_map/ppermute | solution.py:31
  314.0 13.9 %collective-permute-start.14 = (bf16[16,1,34,192]{3,2,1,0:T(8,128)(2,1)S(1)}, bf16[16,1,34,192]{3,2,1,0:T(8,128)(2,1)S(1)}, u32[]{:S(2)}, u32[]{:S(2)}) collective-permute-start(bf16[16,1,34,192]{3,2,1,0:T(8,128)(2,1)S(1)} %get-tuple-element.40), channel_id=1, source_target_pairs={{0,1},{1,2},{2,3},{3,4},{4,5},{5,6},{6,7},{7,8},{8,9},{9,10},{10,1... | collective-permute-start | bytes 626696 | tf_op jit(solution)/shard_map/ppermute | solution.py:31
  320.2 12.1 %collective-permute-start.15 = (bf16[16,1,34,192]{3,2,1,0:T(8,128)(2,1)S(1)}, bf16[16,1,34,192]{3,2,1,0:T(8,128)(2,1)S(1)}, u32[]{:S(2)}, u32[]{:S(2)}) collective-permute-start(bf16[16,1,34,192]{3,2,1,0:T(8,128)(2,1)S(1)} %get-tuple-element.41), channel_id=1, source_target_pairs={{1,0},{2,1},{3,2},{4,3},{5,4},{6,5},{7,6},{8,7},{9,8},{10,9},{11,1... | collective-permute-start | bytes 626696 | tf_op jit(solution)/shard_map/ppermute | solution.py:34
  367.3 6.3 %copy-start.9 = (bf16[16,8,32,192]{3,2,1,0:T(8,128)(2,1)S(1)}, bf16[16,8,32,192]{3,2,1,0:T(8,128)(2,1)}, u32[]{:S(2)}) copy-start(bf16[16,8,32,192]{3,2,1,0:T(8,128)(2,1)} %get-tuple-element.29) | copy-start | bytes 4718596
  385.7 4.2 copy-start.8
  394.4 5.9 %copy-start.7 = (bf16[16,8,32,192]{3,2,1,0:T(8,128)(2,1)S(1)}, bf16[16,8,32,192]{3,2,1,0:T(8,128)(2,1)}, u32[]{:S(2)}) copy-start(bf16[16,8,32,192]{3,2,1,0:T(8,128)(2,1)} %get-tuple-element.22) | copy-start | bytes 4718596
  404.8 5.7 %copy-start.6 = (bf16[16,8,32,192]{3,2,1,0:T(8,128)(2,1)S(1)}, bf16[16,8,32,192]{3,2,1,0:T(8,128)(2,1)}, u32[]{:S(2)}) copy-start(bf16[16,8,32,192]{3,2,1,0:T(8,128)(2,1)} %get-tuple-element.19) | copy-start | bytes 4718596
  414.9 5.7 %copy-start.5 = (bf16[16,8,32,192]{3,2,1,0:T(8,128)(2,1)S(1)}, bf16[16,8,32,192]{3,2,1,0:T(8,128)(2,1)}, u32[]{:S(2)}) copy-start(bf16[16,8,32,192]{3,2,1,0:T(8,128)(2,1)} %get-tuple-element.16) | copy-start | bytes 4718596
  425.1 5.7 %copy-start.4 = (bf16[16,8,32,192]{3,2,1,0:T(8,128)(2,1)S(1)}, bf16[16,8,32,192]{3,2,1,0:T(8,128)(2,1)}, u32[]{:S(2)}) copy-start(bf16[16,8,32,192]{3,2,1,0:T(8,128)(2,1)} %get-tuple-element.14) | copy-start | bytes 4718596
  435.5 5.7 %copy-start.10 = (bf16[16,8,32,192]{3,2,1,0:T(8,128)(2,1)S(1)}, bf16[16,8,32,192]{3,2,1,0:T(8,128)(2,1)}, u32[]{:S(2)}) copy-start(bf16[16,8,32,192]{3,2,1,0:T(8,128)(2,1)} %get-tuple-element.32) | copy-start | bytes 4718596
  445.5 4.1 copy-start.1
  445.5 4.1 copy-start.20
  455.9 5.5 %copy-start.3 = (bf16[8,2,8,6144]{3,2,1,0:T(8,128)(2,1)S(1)}, bf16[8,2,8,6144]{3,2,1,0:T(8,128)(2,1)}, u32[]{:S(2)}) copy-start(bf16[8,2,8,6144]{3,2,1,0:T(8,128)(2,1)} %copy-done.2) | copy-start | bytes 4718596
